TPU v7x, 512 devices: a whole 4x8x8 slice. The times are simulated.
512 devices in a mesh: pair: 64 (over z, x, core), slab: 8 (over y).
Axes of the slice: x: 4, y: 8, z: 8, core: 2. Of those that a mesh axis runs over, the one named last changes fastest.
Arguments:
- amps: bfloat16 [1024, 1024, 128], P(('pair', 'slab')), may hold values from -6 to 6
- symmetry: int32 [1024], replicated, may hold values from 0 to 3
- screen: int32 [64, 16, 16], P('pair'), may hold values 0 or 1
- owner: int32 [1024], replicated, may hold values from 0 to 63, as said below
- integrals: bfloat16 [64, 2048, 2048], P('pair', 'slab'), may hold values from -0.25 to 0.25
Outputs:
- residual: bfloat16 [1024, 64, 16, 128], P(('pair', 'slab'))
Inputs may be any that keep to these rules, and one draw needn't show every extreme that they name: Every owner from 0 to 63 holds exactly 16 tiles.
All inputs are finite; a program needn't handle non-finite values. No bound on the sum of `screen` on one device may be relied on, other than what follows from the above.
Results may differ from a plain program's by a relative error of at most 0.001.
Values may be sent and summed in bfloat16 or wider, within the bound.
A program may use at most 64 MiB of HBM per device.

v0:
```python
import jax
import jax.numpy as jnp
from jax import lax
from jax.sharding import PartitionSpec as P


def contract(operand, block_piece, mask_piece, per_owner, tile_width):
    rows_here = block_piece.shape[0]
    masked = (
        block_piece.reshape(rows_here, per_owner, tile_width) * mask_piece[:, :, None]
    ).reshape(rows_here, per_owner * tile_width)
    return jnp.dot(operand, masked, preferred_element_type=jnp.float32)


def on_device(amps, symmetry, screen, owner, integrals):
    n_pair = lax.axis_size("pair")
    local_rows, tile_count, tile_width = amps.shape
    per_owner = tile_count // n_pair
    owner_span = per_owner * tile_width
    tile_order = jnp.argsort(owner, stable=True).reshape(n_pair, per_owner)
    sorted_amps = jnp.take(amps, tile_order.reshape(-1), axis=1).reshape(
        local_rows, n_pair, owner_span
    )
    owned = lax.dynamic_index_in_dim(tile_order, lax.axis_index("pair"), 0, keepdims=False)
    labels = jnp.take(symmetry, owned)
    allowed = ((labels[:, None] == labels[None, :]) & (screen[0] == 1)).astype(jnp.bfloat16)
    mask_rows = jnp.repeat(allowed, tile_width, axis=0)
    block_rows = integrals[0]
    received = lax.all_to_all(sorted_amps, "pair", split_axis=1, concat_axis=1, tiled=True)
    flat_rows = received.reshape(local_rows * n_pair, owner_span)
    summed = contract(
        flat_rows,
        lax.all_gather(block_rows, "slab", axis=0, tiled=True),
        mask_rows,
        per_owner,
        tile_width,
    )
    product = summed.astype(jnp.bfloat16).reshape(local_rows, n_pair, owner_span)
    returned = lax.all_to_all(product, "pair", split_axis=1, concat_axis=1, tiled=True)
    return returned.reshape(local_rows, n_pair, per_owner, tile_width)


def solution(mesh):
    in_specs = (
        P(("pair", "slab"), None, None),
        P(),
        P("pair", None, None),
        P(),
        P("pair", "slab", None),
    )
    out_specs = P(("pair", "slab"), None, None, None)
    return jax.shard_map(
        on_device, mesh=mesh, in_specs=in_specs, out_specs=out_specs, check_vma=False
    )
```

profile of v0, /device:TPU:1, one launch (start us, length us, event | category | flops | bytes accessed | tf_op | source)
XLA Modules:
  0.0 163.3 jit_solution(9701086411608174818)
XLA Ops:
  6.5 0.0 copy-start
  6.5 0.0 copy-start.1
  6.5 0.0 copy-start.2
  6.5 0.0 all-gather.3.cloned.1.call-start
  6.5 0.7 all-gather.3.cloned.1.call-update
  7.3 5.1 %sort.17 = (s32[1024]{0:T(1024)}, s32[1024]{0:T(1024)S(1)}) sort(s32[1024]{0:T(1024)} %param.8, s32[1024]{0:T(1024)S(1)} %iota.4), dimensions={0}, to_apply=%region_0.0 | sort | flops 10240 | bytes 16384 | tf_op jit(solution)/shard_map/jit(argsort)/sort | solution.py:20
  12.3 0.1 broadcast_in_dim.25
  12.4 0.2 broadcast_in_dim.26
  12.6 0.1 copy.23
  12.7 0.0 copy-done
  12.7 4.4 %gather_fusion = bf16[1024,2,128]{2,0,1:T(8,128)(2,1)S(1)} fusion(bf16[2,1024,128]{2,1,0:T(8,128)(2,1)S(1)} %copy-done, s32[1024]{0:T(1024)S(1)} %fusion.5), kind=kCustom, calls=%fused_computation | custom fusion | bytes 1052672 | tf_op jit(solution)/shard_map/jit(_take)/gather | solution.py:21
  17.1 0.2 gather.13
  17.4 1.9 %broadcast_select_fusion = bf16[2,64,2048]{2,0,1:T(2,128)(2,1)} fusion(pred[64,2048]{1,0:T(8,128)(4,1)S(1)} %bitcast.43, bf16[2,64,2048]{2,1,0:T(8,128)(2,1)S(1)} %gather.13), kind=kLoop, calls=%fused_computation.7 | loop fusion | flops 262144 | bytes 1179648 | tf_op jit(solution)/shard_map/jit(_take)/select_n | solution.py:21
  19.2 14.8 %all-to-all-start = ((bf16[2,64,2048]{2,0,1:T(2,128)(2,1)}), bf16[2,64,2048]{2,0,1:T(2,128)(2,1)S(1)}, u32[]{:S(2)}, u32[]{:S(2)}) async-start(bf16[2,64,2048]{2,0,1:T(2,128)(2,1)} %broadcast_select_fusion), calls=%async_computation | async-start | bytes 1048576 | tf_op jit(solution)/shard_map/all_to_all | solution.py:29
  34.1 0.1 reshape.78
  34.2 0.0 copy-done.1
  34.2 0.6 gather_fusion.1
  34.9 0.0 copy-done.2
  34.9 0.1 fusion.4
  35.0 16.8 %all-to-all-done = bf16[2,64,2048]{2,0,1:T(2,128)(2,1)S(1)} async-done(((bf16[2,64,2048]{2,0,1:T(2,128)(2,1)}), bf16[2,64,2048]{2,0,1:T(2,128)(2,1)S(1)}, u32[]{:S(2)}, u32[]{:S(2)}) %all-to-all-start) | async-done | bytes 524320 | tf_op jit(solution)/shard_map/all_to_all | solution.py:29
  51.8 0.2 copy.10
  52.0 59.5 %all-gather.3.cloned.1.call-done = bf16[1,2048,2048]{2,1,0:T(8,128)(2,1)} async-done(((bf16[1,256,2048]{2,1,0:T(8,128)(2,1)}), bf16[1,2048,2048]{2,1,0:T(8,128)(2,1)}) %all-gather.3.cloned.1.call-update) | async-done | bytes 8388624 | tf_op jit(solution)/shard_map/all_gather | solution.py:33
  111.5 0.0 copy-start.3
  111.5 0.1 broadcast_in_dim.31
  111.5 9.0 %mul.14 = bf16[2048,16,128]{2,1,0:T(8,128)(2,1)S(1)} broadcast(bf16[2048,16]{1,0:T(8,128)(2,1)S(1)} %bitcast.41), dimensions={0,1} | broadcast | bytes 8454144 | tf_op jit(solution)/shard_map/mul | solution.py:10
  120.5 0.0 copy-done.3
  120.5 5.7 %fusion.3 = bf16[128,2048]{1,0:T(8,128)(2,1)S(1)} fusion(bf16[128,2048]{1,0:T(8,128)(2,1)S(1)} %bitcast.44, bf16[256,8,16,128]{3,2,1,0:T(8,128)(2,1)S(1)} %bitcast.40, bf16[1,2048,2048]{2,1,0:T(8,128)(2,1)S(1)} %copy-done.3), kind=kOutput, calls=%fused_computation.6 | convolution fusion | flops 1078198272 | bytes 17825792 | tf_op jit(solution)/shard_map/dot_general | solution.py:12
  126.2 0.5 copy.11
  126.7 28.5 %all_to_all.10 = bf16[2,64,2048]{2,0,1:T(2,128)(2,1)S(1)} all-to-all(bf16[2,64,2048]{2,0,1:T(2,128)(2,1)S(1)} %copy.11), channel_id=1, replica_groups=mesh['pair'=64,'slab'=8] {'pair'}, dimensions={1} | all-to-all | bytes 1048576 | tf_op jit(solution)/shard_map/all_to_all | solution.py:39
  155.3 0.3 reshape.80
  155.6 0.8 copy.12
  (7 shorter events, 0.1 us)
Async XLA Ops:
  6.5 6.2 %copy-start = (bf16[2,1024,128]{2,1,0:T(8,128)(2,1)S(1)}, bf16[2,1024,128]{2,1,0:T(8,128)(2,1)}, u32[]{:S(2)}) copy-start(bf16[2,1024,128]{2,1,0:T(8,128)(2,1)} %param.5) | copy-start | bytes 1572868
  6.5 27.7 %copy-start.1 = (s32[1024]{0:T(1024)S(1)}, s32[1024]{0:T(1024)}, u32[]{:S(2)}) copy-start(s32[1024]{0:T(1024)} %param.6) | copy-start | bytes 12292
  6.5 28.3 %copy-start.2 = (s32[1,16,16]{2,1,0:T(8,128)S(1)}, s32[1,16,16]{2,1,0:T(8,128)}, u32[]{:S(2)}) copy-start(s32[1,16,16]{2,1,0:T(8,128)} %param.7) | copy-start | bytes 3076
  6.5 104.9 %all-gather.3.cloned.1.call-start = ((), (), s32[]{:S(2)}) async-start(), calls=%async_computation.2 | async-start | bytes 9437184 | tf_op jit(solution)/shard_map/all_gather | solution.py:33
  19.2 32.6 %all-to-all-start = ((bf16[2,64,2048]{2,0,1:T(2,128)(2,1)}), bf16[2,64,2048]{2,0,1:T(2,128)(2,1)S(1)}, u32[]{:S(2)}, u32[]{:S(2)}) async-start(bf16[2,64,2048]{2,0,1:T(2,128)(2,1)} %broadcast_select_fusion), calls=%async_computation | async-start | bytes 1048576 | tf_op jit(solution)/shard_map/all_to_all | solution.py:29
  111.5 9.0 %copy-start.3 = (bf16[1,2048,2048]{2,1,0:T(8,128)(2,1)S(1)}, bf16[1,2048,2048]{2,1,0:T(8,128)(2,1)}, u32[]{:S(2)}) copy-start(bf16[1,2048,2048]{2,1,0:T(8,128)(2,1)} %all-gather.3.cloned.1.call-done) | copy-start | bytes 25165828
Sparse Core Ops, SparseCore 0:
  9.4 101.9 all-gather.2
where the time goes:
time: 164 us; the launch traced here: 163 us
  waiting for transfers between devices  77 us (47%)
  blocking collectives  28.5 us (17%)
  local copies, waits for them, and re-layouts  16.6 us (10%)
  starting transfers between devices  14.8 us (9%)
  between operations  13.6 us (8%)
  other arithmetic  7.06 us (4%)
  matrix products  5.67 us (3%)
    all_gather x1, waiting for transfers between devices, on_device(): lax.all_gather(block_rows, 'slab', axis=0, tiled=True)  59.5 us
    all_to_all x1, blocking collectives, on_device(): lax.all_to_all(product, 'pair', split_axis=1, concat_axis=1, tiled=True)  28.5 us
    all_to_all x1, waiting for transfers between devices, on_device(): lax.all_to_all(sorted_amps, 'pair', split_axis=1, concat_axis=1, tiled=True)  16.8 us
    all_to_all x1, starting transfers between devices, on_device(): lax.all_to_all(sorted_amps, 'pair', split_axis=1, concat_axis=1, tiled=True)  14.8 us
    mul x1, local copies, waits for them, and re-layouts, contract(): block_piece.reshape(rows_here, per_owner, tile_width)  8.96 us
    dot_general x1, matrix products, contract(): return jnp.dot(operand, masked, preferred_element_type=jnp.float32)  5.67 us
    sort x1, other arithmetic, on_device(): tile_order = jnp.argsort(owner, stable=True).reshape(n_pair, per_owner)  5.05 us
    gather x2, local copies, waits for them, and re-layouts, on_device(): jnp.take(amps, tile_order.reshape(-1), axis=1)  4.62 us
  transfers between devices with their start and end apart: 2, of which 2 were waited for; matrix products, arithmetic and copies ran while one was open for 8% of the time, Pallas kernels for 0%

commit v1 on v0

v1 whole, which is shorter than its diff:
```python
import functools

import jax
import jax.numpy as jnp
from jax import lax
from jax.experimental import pallas as pl
from jax.experimental.pallas import tpu as pltpu
from jax.sharding import PartitionSpec as P

MESH = pl.DeviceIdType.MESH
CHUNKS = 4


def one_hot_bf16(cond):
    return jnp.where(cond, 1.0, 0.0).astype(jnp.bfloat16)


def kernel(
    n_pair,
    n_slab,
    owner_ref,
    sym_ref,
    screen_ref,
    amps_ref,
    b_ref,
    out_ref,
    send_a,
    recv_a,
    a_mat,
    f32_buf,
    gathered,
    mask_ref,
    send_c,
    ring_send,
    ring_recv,
    a_send,
    a_recv,
    c_send,
    c_recv,
):
    pair = lax.axis_index("pair")
    slab = lax.axis_index("slab")
    rows, tiles, width = amps_ref.shape
    per = tiles // n_pair
    depth, cols = b_ref.shape
    chunk = cols // CHUNKS
    up = lax.rem(slab + 1, n_slab)
    down = lax.rem(slab + n_slab - 1, n_slab)
    toward = ((up, 1), (down, -1))

    barrier = pltpu.get_barrier_semaphore()

    @pl.loop(1, n_pair)
    def _(i):
        other = lax.rem(pair + i, n_pair)
        pl.semaphore_signal(barrier, inc=1, device_id=(other, slab), device_id_type=MESH)

    for there, _ in toward:
        pl.semaphore_signal(barrier, inc=1, device_id=(pair, there), device_id_type=MESH)
    pl.semaphore_wait(barrier, n_pair - 1 + 2)

    half = n_slab // 2

    def steps_of(c, way):
        return half if (c + way) % 2 == 0 else half - 1

    def hop(step, c, way):
        there, sign = toward[way]
        block = lax.rem(slab - sign * step + n_slab, n_slab)
        src = b_ref.at[:, pl.ds(c * chunk, chunk)] if step == 0 else gathered.at[block, c]
        return pltpu.make_async_remote_copy(
            src_ref=src,
            dst_ref=gathered.at[block, c],
            send_sem=ring_send.at[way, step, c],
            recv_sem=ring_recv.at[way, step, c],
            device_id=(pair, there),
            device_id_type=MESH,
        )

    def advance(step):
        for c in range(CHUNKS):
            for way in range(2):
                if step < steps_of(c, way):
                    if step:
                        hop(step - 1, c, way).wait_recv()
                    hop(step, c, way).start()

    advance(0)
    for c in range(CHUNKS):
        gathered[slab, c] = b_ref[:, c * chunk : (c + 1) * chunk]

    owned = owner_ref[...]
    sel = lax.broadcasted_iota(jnp.int32, (n_pair, tiles), 0) == owned
    sel_bf = one_hot_bf16(sel)
    count = jnp.zeros((n_pair, tiles), jnp.float32)
    span = 256
    for part in range(tiles // span):
        before = lax.broadcasted_iota(jnp.int32, (span, tiles), 0) + part * span < lax.broadcasted_iota(
            jnp.int32, (span, tiles), 1
        )
        count += jnp.dot(
            sel_bf[:, part * span : (part + 1) * span], one_hot_bf16(before), preferred_element_type=jnp.float32
        )
    base = (lax.broadcasted_iota(jnp.int32, (n_pair, tiles), 0) * per).astype(jnp.float32)
    rank = jnp.sum(jnp.where(sel, count + base, 0.0), axis=0, keepdims=True).astype(jnp.int32)

    flat = jnp.concatenate([amps_ref[o] for o in range(rows)], axis=1)
    for part in range(tiles // span):
        pick = one_hot_bf16(lax.broadcasted_iota(jnp.int32, (span, tiles), 0) + part * span == rank)
        got = jnp.dot(pick, flat, preferred_element_type=jnp.float32).astype(jnp.bfloat16)
        first = part * span // per
        for o in range(rows):
            send_a[first : first + span // per, o] = got[:, o * width : (o + 1) * width].reshape(
                span // per, per, width
            )

    def a_copy(i):
        other = lax.rem(pair + i, n_pair)
        return pltpu.make_async_remote_copy(
            src_ref=send_a.at[other],
            dst_ref=recv_a.at[pair],
            send_sem=a_send,
            recv_sem=a_recv,
            device_id=(other, slab),
            device_id_type=MESH,
        )

    @pl.loop(1, n_pair)
    def _(i):
        a_copy(i).start()

    recv_a[pair] = send_a[pair]

    mine = one_hot_bf16(lax.broadcasted_iota(jnp.int32, (per, tiles), 0) + pair * per == rank)
    classes = lax.broadcasted_iota(jnp.int32, (128, tiles), 0) == sym_ref[...]
    labels = lax.dot_general(
        mine, one_hot_bf16(classes), (((1,), (1,)), ((), ())), preferred_element_type=jnp.float32
    ).astype(jnp.bfloat16)
    same = lax.dot_general(labels, labels, (((1,), (1,)), ((), ())), preferred_element_type=jnp.float32)
    allowed = jnp.where(screen_ref[...] == 1, same, 0.0).astype(jnp.bfloat16)
    spread = one_hot_bf16(
        lax.broadcasted_iota(jnp.int32, (per, cols), 0) == lax.broadcasted_iota(jnp.int32, (per, cols), 1) // width
    )
    mask_ref[...] = jnp.dot(allowed, spread, preferred_element_type=jnp.float32)

    for step in range(1, half):
        advance(step)

    def all_of(ref, sem):
        part = ref.at[pl.ds(0, n_pair - 1)]
        return pltpu.make_async_copy(part, part, sem)

    all_of(recv_a, a_recv).wait()
    f32_buf[...] = recv_a[...].reshape(n_pair * rows * per, width).astype(jnp.float32)
    held = n_pair * rows
    for k in range(per):
        a_mat[:, k * width : (k + 1) * width] = f32_buf[pl.ds(k, held, stride=per), :].astype(jnp.bfloat16)

    for c in range(CHUNKS):
        for way in range(2):
            hop(steps_of(c, way) - 1, c, way).wait_recv()
        acc = None
        for y in range(n_slab):
            term = []
            for part in range(depth // width):
                k = y * (depth // width) + part
                row = mask_ref[k : k + 1, c * chunk : (c + 1) * chunk].astype(jnp.bfloat16)
                term.append(gathered[y, c, part * width : (part + 1) * width, :] * row)
            prod = jnp.dot(
                a_mat[:, y * depth : (y + 1) * depth],
                jnp.concatenate(term, axis=0),
                preferred_element_type=jnp.float32,
            )
            acc = prod if acc is None else acc + prod
        for part in range(chunk // width):
            l = c * (chunk // width) + part
            f32_buf[pl.ds(l, held, stride=per), :] = acc[:, part * width : (part + 1) * width]

    send_c[...] = f32_buf[...].astype(jnp.bfloat16).reshape(n_pair, rows, per, width)

    def c_copy(i):
        other = lax.rem(pair + i, n_pair)
        return pltpu.make_async_remote_copy(
            src_ref=send_c.at[other],
            dst_ref=out_ref.at[:, pair],
            send_sem=c_send,
            recv_sem=c_recv,
            device_id=(other, slab),
            device_id_type=MESH,
        )

    @pl.loop(1, n_pair)
    def _(i):
        c_copy(i).start()

    out_ref[:, pair] = send_c[pair]

    for step in range(half):
        for c in range(CHUNKS):
            for way in range(2):
                if step < steps_of(c, way):
                    hop(step, c, way).wait_send()
    all_of(send_a, a_send).wait()
    all_of(send_c, c_send).wait()
    all_of(send_c, c_recv).wait()


def on_device(amps, symmetry, screen, owner, integrals):
    n_pair, n_slab = lax.axis_size("pair"), lax.axis_size("slab")
    rows, tiles, width = amps.shape
    per = tiles // n_pair
    depth, cols = integrals.shape[1:]
    bf16 = jnp.bfloat16
    vmem = pl.BlockSpec(memory_space=pltpu.VMEM)
    return pl.pallas_call(
        functools.partial(kernel, n_pair, n_slab),
        out_shape=jax.ShapeDtypeStruct((rows, n_pair, per, width), bf16),
        in_specs=[vmem] * 5,
        out_specs=vmem,
        scratch_shapes=[
            pltpu.VMEM((n_pair, rows, per, width), bf16),
            pltpu.VMEM((n_pair, rows, per, width), bf16),
            pltpu.VMEM((n_pair * rows, per * width), bf16),
            pltpu.VMEM((n_pair * rows * per, width), jnp.float32),
            pltpu.VMEM((n_slab, CHUNKS, depth, cols // CHUNKS), bf16),
            pltpu.VMEM((per, cols), jnp.float32),
            pltpu.VMEM((n_pair, rows, per, width), bf16),
            pltpu.SemaphoreType.DMA((2, n_slab // 2, CHUNKS)),
            pltpu.SemaphoreType.DMA((2, n_slab // 2, CHUNKS)),
            pltpu.SemaphoreType.DMA,
            pltpu.SemaphoreType.DMA,
            pltpu.SemaphoreType.DMA,
            pltpu.SemaphoreType.DMA,
        ],
        compiler_params=pltpu.CompilerParams(
            collective_id=0, has_side_effects=True, vmem_limit_bytes=40 << 20
        ),
    )(owner[None, :], symmetry[None, :], screen[0], amps, integrals[0])


def solution(mesh):
    in_specs = (
        P(("pair", "slab"), None, None),
        P(),
        P("pair", None, None),
        P(),
        P("pair", "slab", None),
    )
    out_specs = P(("pair", "slab"), None, None, None)
    return jax.shard_map(
        on_device, mesh=mesh, in_specs=in_specs, out_specs=out_specs, check_vma=False
    )
```

time: 164 us -> 117 us (0.71)
  Pallas kernels: 0 us -> 112 us
  waiting for transfers between devices: 77 us -> 0 us
  blocking collectives: 28.5 us -> 0 us
  starting transfers between devices: 14.8 us -> 0 us
  between operations: 13.6 us -> 0.01 us
  local copies, waits for them, and re-layouts: 16.6 us -> 5.13 us
  other arithmetic: 7.06 us -> 0 us
  matrix products: 5.67 us -> 0 us
    pallas_call x0 -> x1, Pallas kernels: none -> 112 us  [on_device(): pl.pallas_call(functools.partial(kernel, n_pair, n_slab), out_shape=jax.S...]
    all_gather x1 -> x0, waiting for transfers between devices: 59.5 us -> none  [on_device(): lax.all_gather(block_rows, 'slab', axis=0, tiled=True)]
    all_to_all x1 -> x0, blocking collectives: 28.5 us -> none  [on_device(): lax.all_to_all(product, 'pair', split_axis=1, concat_axis=1, tiled=True)]
    all_to_all x1 -> x0, waiting for transfers between devices: 16.8 us -> none  [on_device(): lax.all_to_all(sorted_amps, 'pair', split_axis=1, concat_axis=1, tiled=True)]
    all_to_all x1 -> x0, starting transfers between devices: 14.8 us -> none  [on_device(): lax.all_to_all(sorted_amps, 'pair', split_axis=1, concat_axis=1, tiled=True)]
    mul x1 -> x0, local copies, waits for them, and re-layouts: 8.96 us -> none  [contract(): block_piece.reshape(rows_here, per_owner, tile_width)]
    dot_general x1 -> x0, matrix products: 5.67 us -> none  [contract(): return jnp.dot(operand, masked, preferred_element_type=jnp.float32)]
    gather x3 -> x0, local copies, waits for them, and re-layouts: 5.26 us -> none  [the longest x2 4.62 us: on_device(): jnp.take(amps, tile_order.reshape(-1), axis=1)]
  transfers between devices with their start and end apart: 2 -> 0, of which waited for: 2 -> 0; matrix products, arithmetic and copies ran while one was open for 8% -> 0% of each run, Pallas kernels for 0% -> 0%
where the time goes in v1:
time: 117 us
  Pallas kernels  112 us (96%)
  local copies, waits for them, and re-layouts  5.13 us (4%)
    pallas_call x1, Pallas kernels, on_device(): pl.pallas_call(functools.partial(kernel, n_pair, n_slab), out_shape=jax.S...  112 us
    unnamed x11, local copies, waits for them, and re-layouts  5.13 us

profile of v1, /device:TPU:1, one launch (start us, length us, event | category | flops | bytes accessed | tf_op | source)
XLA Modules:
  0.0 117.0 jit_solution(18248100878073109322)
XLA Ops:
  0.0 0.0 copy-start.3
  0.0 0.7 copy-done.3
  0.7 0.0 copy-start
  0.7 1.2 %copy-done = bf16[1,256,2048]{2,1,0:T(8,128)(2,1)S(1)} copy-done((bf16[1,256,2048]{2,1,0:T(8,128)(2,1)S(1)}, bf16[1,256,2048]{2,1,0:T(8,128)(2,1)}, u32[]{:S(2)}) %copy-start) | copy-done | bytes 1048600
  1.9 0.0 copy-start.1
  1.9 1.0 copy-done.1
  3.0 0.0 copy-start.2
  3.0 0.7 copy-done.2
  3.7 0.0 copy-start.4
  3.7 0.7 copy-done.4
  4.3 111.9 %shard_map.55 = bf16[2,64,16,128]{3,2,1,0:T(8,128)(2,1)S(1)} custom-call(s32[1,1024]{1,0:T(1,128)S(1)} %bitcast.6, s32[1,1024]{1,0:T(1,128)S(1)} %bitcast.7, s32[16,16]{1,0:T(8,128)S(1)} %bitcast.5, bf16[2,1024,128]{2,1,0:T(8,128)(2,1)S(1)} %copy-done.1, bf16[256,2048]{1,0:T(8,128)(2,1)S(1)} %bitcast.4), custom_call_target="tpu_custom_call" | custom-call | tf_op jit(solution)/shard_map/pallas_call | solution.py:215
  116.2 0.8 copy.7
Async XLA Ops:
  0.0 0.7 copy-start.3
  0.7 1.2 %copy-start = (bf16[1,256,2048]{2,1,0:T(8,128)(2,1)S(1)}, bf16[1,256,2048]{2,1,0:T(8,128)(2,1)}, u32[]{:S(2)}) copy-start(bf16[1,256,2048]{2,1,0:T(8,128)(2,1)} %param.9) | copy-start | bytes 3145732
  1.9 1.0 copy-start.1
  3.0 0.7 copy-start.2
  3.7 0.7 copy-start.4

commit v2 on v1

v2 whole, which is shorter than its diff:
```python
import functools

import jax
import jax.numpy as jnp
from jax import lax
from jax.experimental import pallas as pl
from jax.experimental.pallas import tpu as pltpu
from jax.sharding import PartitionSpec as P

MESH = pl.DeviceIdType.MESH
CORES = 2
RING = 4
ROW = CORES * RING
RELAY = 128


def one_hot_bf16(cond):
    return jnp.where(cond, 1.0, 0.0).astype(jnp.bfloat16)


def kernel(
    n_pair,
    n_slab,
    owner_hbm,
    sym_hbm,
    screen_hbm,
    amps_hbm,
    b_hbm,
    out_ref,
    owner_ref,
    sym_ref,
    screen_ref,
    amps_ref,
    send_a,
    recv_a,
    a_mat,
    f32_buf,
    acc,
    gathered,
    coupling,
    mask_ref,
    send_c,
    load_sem,
    first_send,
    first_recv,
    side_send,
    side_recv,
    relay_send,
    relay_recv,
    twin_send,
    twin_recv,
    screen_send,
    screen_recv,
    a_send,
    a_recv,
    c_send,
    c_recv,
):
    pair = lax.axis_index("pair")
    slab = lax.axis_index("slab")
    rows, tiles, width = amps_hbm.shape
    per = tiles // n_pair
    depth, cols = b_hbm.shape
    piece = cols // ROW
    layer = pair // ROW
    ring = lax.rem(pair // CORES, RING)
    core = lax.rem(pair, CORES)
    row_base = layer * ROW

    home = ring + RING * core
    served = row_base + lax.rem(slab, RING) * CORES + slab // RING
    spot = layer * n_slab + slab

    loads = [
        pltpu.make_async_copy(src, dst, load_sem.at[i])
        for i, (src, dst) in enumerate(
            ((owner_hbm, owner_ref), (sym_hbm, sym_ref), (screen_hbm, screen_ref), (amps_hbm, amps_ref))
        )
    ]
    for load in loads:
        load.start()

    def in_row(i):
        return row_base + lax.rem(pair - row_base + i, ROW)

    def spread_over(i):
        other = lax.rem(spot + i, n_pair)
        there = other // n_slab
        return there * ROW + pair - row_base, lax.rem(other, n_slab)

    barrier = pltpu.get_barrier_semaphore()

    @pl.loop(1, n_pair)
    def _(i):
        pl.semaphore_signal(barrier, inc=1, device_id=spread_over(i), device_id_type=MESH)

    @pl.loop(1, ROW)
    def _(i):
        pl.semaphore_signal(barrier, inc=1, device_id=(in_row(i), slab), device_id_type=MESH)

    @pl.loop(1, n_slab)
    def _(i):
        pl.semaphore_signal(barrier, inc=1, device_id=(served, lax.rem(slab + i, n_slab)), device_id_type=MESH)

    at_home = home == slab

    peers = n_pair - 1 + ROW - 1 + ROW - 1

    @pl.when(at_home)
    def _():
        pl.semaphore_wait(barrier, peers)

    @pl.when(jnp.logical_not(at_home))
    def _():
        pl.semaphore_signal(barrier, inc=1, device_id=(served, slab), device_id_type=MESH)
        pl.semaphore_wait(barrier, peers + 1)

    def first_copy(i):
        other = in_row(i)
        q = other - row_base
        return pltpu.make_async_remote_copy(
            src_ref=b_hbm.at[:, pl.ds(pl.multiple_of(q * piece, piece), piece)],
            dst_ref=gathered.at[slab, q],
            send_sem=first_send,
            recv_sem=first_recv.at[slab],
            device_id=(other, home),
            device_id_type=MESH,
        )

    me = pair - row_base
    own_piece = pltpu.make_async_copy(
        b_hbm.at[:, pl.ds(pl.multiple_of(me * piece, piece), piece)], gathered.at[slab, me], first_recv.at[slab]
    )

    @pl.loop(1, ROW)
    def _(i):
        first_copy(i).start()

    @pl.when(at_home)
    def _():
        own_piece.start()

    @pl.when(jnp.logical_not(at_home))
    def _():
        first_copy(0).start()

    right = row_base + lax.rem(ring + 1, RING) * CORES + core
    left = row_base + lax.rem(ring + RING - 1, RING) * CORES + core
    twin = row_base + ring * CORES + 1 - core
    q_me = me
    q_right, q_left = right - row_base, left - row_base
    q_far = lax.rem(ring + 2, RING) * CORES + core
    order = [0]
    for k in range(1, n_slab // 2):
        order += [k, n_slab - k]
    order += [n_slab // 2]

    def source_of(t):
        return lax.rem(slab + order[t], n_slab)

    def remote(ref, send, recv, to):
        return pltpu.make_async_remote_copy(
            src_ref=ref, dst_ref=ref, send_sem=send, recv_sem=recv, device_id=(to, slab), device_id_type=MESH
        )

    def side(t, way):
        y = source_of(t)
        return remote(gathered.at[y, q_me], side_send.at[way, t], side_recv.at[way, t], (right, left)[way])

    def relay(t, way):
        y = source_of(t)
        part = pl.ds(0, RELAY) if way == 0 else pl.ds(RELAY, depth - RELAY)
        ref = gathered.at[y, (q_left, q_right)[way], part]
        return remote(ref, relay_send.at[way, t], relay_recv.at[way, t], (right, left)[way])

    def across(t, q):
        y = source_of(t)
        return remote(gathered.at[y, q], twin_send.at[t], twin_recv.at[t], twin)

    def bytes_of(t, sem):
        ref = gathered.at[source_of(t), pl.ds(0, RING)]
        return pltpu.make_async_copy(ref, ref, sem)

    def stage0(t):
        y = source_of(t)
        pltpu.make_async_copy(gathered.at[y, q_me], gathered.at[y, q_me], first_recv.at[y]).wait()
        side(t, 0).start()
        side(t, 1).start()
        across(t, q_me).start()

    def stage1(t):
        side(t, 0).wait_recv()
        relay(t, 0).start()
        side(t, 1).wait_recv()
        relay(t, 1).start()
        across(t, q_left).start()
        across(t, q_right).start()

    def stage2(t):
        relay(t, 0).wait_recv()
        relay(t, 1).wait_recv()
        across(t, q_far).start()

    for load in loads:
        load.wait()
    owned = owner_ref[...]
    sel = lax.broadcasted_iota(jnp.int32, (n_pair, tiles), 0) == owned
    sel_bf = one_hot_bf16(sel)
    count = jnp.zeros((n_pair, tiles), jnp.float32)
    span = 256
    for part in range(tiles // span):
        before = lax.broadcasted_iota(jnp.int32, (span, tiles), 0) + part * span < lax.broadcasted_iota(
            jnp.int32, (span, tiles), 1
        )
        count += jnp.dot(
            sel_bf[:, part * span : (part + 1) * span], one_hot_bf16(before), preferred_element_type=jnp.float32
        )
    base = (lax.broadcasted_iota(jnp.int32, (n_pair, tiles), 0) * per).astype(jnp.float32)
    rank = jnp.sum(jnp.where(sel, count + base, 0.0), axis=0, keepdims=True).astype(jnp.int32)

    flat = jnp.concatenate([amps_ref[o] for o in range(rows)], axis=1)
    for part in range(tiles // span):
        pick = one_hot_bf16(lax.broadcasted_iota(jnp.int32, (span, tiles), 0) + part * span == rank)
        got = jnp.dot(pick, flat, preferred_element_type=jnp.float32).astype(jnp.bfloat16)
        first = part * span // per
        for o in range(rows):
            send_a[first : first + span // per, o] = got[:, o * width : (o + 1) * width].reshape(
                span // per, per, width
            )

    def a_copy(i):
        to, there = spread_over(i)
        wanted = to - (pair - row_base) + lax.rem(there, RING) * CORES + there // RING
        return pltpu.make_async_remote_copy(
            src_ref=send_a.at[wanted],
            dst_ref=recv_a.at[spot],
            send_sem=a_send,
            recv_sem=a_recv,
            device_id=(to, there),
            device_id_type=MESH,
        )

    @pl.loop(1, n_pair)
    def _(i):
        a_copy(i).start()

    recv_a[spot] = send_a[served]

    def screen_copy(i):
        return pltpu.make_async_remote_copy(
            src_ref=coupling,
            dst_ref=coupling,
            send_sem=screen_send,
            recv_sem=screen_recv,
            device_id=(in_row(i), slab),
            device_id_type=MESH,
        )

    @pl.when(at_home)
    def _():
        coupling[...] = jnp.zeros_like(coupling)
        coupling[:, :per] = jnp.where(screen_ref[...] == 1, 1.0, 0.0)

        @pl.loop(1, ROW)
        def _(i):
            screen_copy(i).start()

    stage0(0)
    stage0(1)
    stage1(0)

    @pl.when(jnp.logical_not(at_home))
    def _():
        screen_copy(0).wait_recv()

    mine = one_hot_bf16(lax.broadcasted_iota(jnp.int32, (per, tiles), 0) + served * per == rank)
    classes = lax.broadcasted_iota(jnp.int32, (128, tiles), 0) == sym_ref[...]
    labels = lax.dot_general(
        mine, one_hot_bf16(classes), (((1,), (1,)), ((), ())), preferred_element_type=jnp.float32
    ).astype(jnp.bfloat16)
    same = lax.dot_general(labels, labels, (((1,), (1,)), ((), ())), preferred_element_type=jnp.float32)
    allowed = (coupling[:, :per] * same).astype(jnp.bfloat16)
    spread = one_hot_bf16(
        lax.broadcasted_iota(jnp.int32, (per, cols), 0) == lax.broadcasted_iota(jnp.int32, (per, cols), 1) // width
    )
    mask_ref[...] = jnp.dot(allowed, spread, preferred_element_type=jnp.float32)

    held = n_pair * rows

    def all_of(ref, sem):
        part = ref.at[pl.ds(0, n_pair - 1)]
        return pltpu.make_async_copy(part, part, sem)

    def arrange():
        all_of(recv_a, a_recv).wait()
        f32_buf[...] = recv_a[...].reshape(held * per, width).astype(jnp.float32)
        for k in range(per):
            a_mat[k // 2, :, (k % 2) * width : (k % 2 + 1) * width] = f32_buf[
                pl.ds(k, held, stride=per), :
            ].astype(jnp.bfloat16)

    def multiply(t):
        y = source_of(t)
        bytes_of(t, twin_recv.at[t]).wait()
        lhs = a_mat[y]
        for q in range(ROW):
            term = []
            for part in range(depth // width):
                row = mask_ref[pl.ds(y * (depth // width) + part, 1), q * piece : (q + 1) * piece]
                term.append(gathered[y, q, part * width : (part + 1) * width, :] * row.astype(jnp.bfloat16))
            prod = jnp.dot(lhs, jnp.concatenate(term, axis=0), preferred_element_type=jnp.float32)
            where = slice(q * piece, (q + 1) * piece)
            if t:
                prod = acc[:, where] + prod
            if t < n_slab - 1:
                acc[:, where] = prod
            else:
                for part in range(piece // width):
                    l = q * (piece // width) + part
                    f32_buf[pl.ds(l, held, stride=per), :] = prod[:, part * width : (part + 1) * width]

    for t in range(2, n_slab + 3):
        if t < n_slab:
            stage0(t)
        if t - 1 < n_slab:
            stage1(t - 1)
        if t - 2 < n_slab:
            stage2(t - 2)
        if t == 3:
            arrange()
        if t >= 3:
            multiply(t - 3)

    send_c[...] = f32_buf[...].astype(jnp.bfloat16).reshape(n_pair, rows, per, width)

    def c_copy(i):
        to = spread_over(i)
        return pltpu.make_async_remote_copy(
            src_ref=send_c.at[lax.rem(spot + i, n_pair)],
            dst_ref=out_ref.at[:, served],
            send_sem=c_send,
            recv_sem=c_recv,
            device_id=to,
            device_id_type=MESH,
        )

    @pl.loop(1, n_pair)
    def _(i):
        c_copy(i).start()

    out_ref[:, served] = send_c[spot]

    first_bytes = pltpu.make_async_copy(
        gathered.at[0, pl.ds(0, ROW - 1)], gathered.at[0, pl.ds(0, ROW - 1)], first_send
    )
    first_bytes.wait()

    @pl.when(jnp.logical_not(at_home))
    def _():
        pltpu.make_async_copy(gathered.at[0, 0], gathered.at[0, 0], first_send).wait()

    @pl.when(at_home)
    def _():
        @pl.loop(1, ROW)
        def _(i):
            screen_copy(i).wait_send()

    for t in range(n_slab):
        for way in range(2):
            side(t, way).wait_send()
            relay(t, way).wait_send()
        bytes_of(t, twin_send.at[t]).wait()
    all_of(send_a, a_send).wait()
    all_of(send_c, c_send).wait()
    all_of(send_c, c_recv).wait()


def on_device(amps, symmetry, screen, owner, integrals):
    n_pair, n_slab = lax.axis_size("pair"), lax.axis_size("slab")
    rows, tiles, width = amps.shape
    per = tiles // n_pair
    depth, cols = integrals.shape[1:]
    bf16 = jnp.bfloat16
    dma = pltpu.SemaphoreType.DMA
    return pl.pallas_call(
        functools.partial(kernel, n_pair, n_slab),
        out_shape=jax.ShapeDtypeStruct((rows, n_pair, per, width), bf16),
        in_specs=[pl.BlockSpec(memory_space=pl.ANY)] * 5,
        out_specs=pl.BlockSpec(memory_space=pltpu.VMEM),
        scratch_shapes=[
            pltpu.VMEM((1, tiles), jnp.int32),
            pltpu.VMEM((1, tiles), jnp.int32),
            pltpu.VMEM((per, per), jnp.int32),
            pltpu.VMEM((rows, tiles, width), bf16),
            pltpu.VMEM((n_pair, rows, per, width), bf16),
            pltpu.VMEM((n_pair, rows, per, width), bf16),
            pltpu.VMEM((n_slab, n_pair * rows, depth), bf16),
            pltpu.VMEM((n_pair * rows * per, width), jnp.float32),
            pltpu.VMEM((n_pair * rows, cols), jnp.float32),
            pltpu.VMEM((n_slab, ROW, depth, cols // ROW), bf16),
            pltpu.VMEM((per, 128), jnp.float32),
            pltpu.VMEM((per, cols), jnp.float32),
            pltpu.VMEM((n_pair, rows, per, width), bf16),
            dma((4,)),
            dma,
            dma((n_slab,)),
            dma((2, n_slab)),
            dma((2, n_slab)),
            dma((2, n_slab)),
            dma((2, n_slab)),
            dma((n_slab,)),
            dma((n_slab,)),
            dma,
            dma,
            dma,
            dma,
            dma,
            dma,
        ],
        compiler_params=pltpu.CompilerParams(
            collective_id=0, has_side_effects=True, vmem_limit_bytes=48 << 20
        ),
    )(owner[None, :], symmetry[None, :], screen[0], amps, integrals[0])


def solution(mesh):
    in_specs = (
        P(("pair", "slab"), None, None),
        P(),
        P("pair", None, None),
        P(),
        P("pair", "slab", None),
    )
    out_specs = P(("pair", "slab"), None, None, None)
    return jax.shard_map(
        on_device, mesh=mesh, in_specs=in_specs, out_specs=out_specs, check_vma=False
    )
```

time: 117 us -> 130 us (1.11)
  Pallas kernels: 112 us -> 124 us
    pallas_call x1, Pallas kernels: 112 us -> 124 us  [on_device(): pl.pallas_call(functools.partial(kernel, n_pair, n_slab), out_shape=jax.S...]
where the time goes in v2:
time: 130 us; the launch traced here: 129 us
  Pallas kernels  124 us (95%)
  local copies, waits for them, and re-layouts  5.13 us (4%)
    pallas_call x1, Pallas kernels, on_device(): pl.pallas_call(functools.partial(kernel, n_pair, n_slab), out_shape=jax.S...  124 us
    unnamed x11, local copies, waits for them, and re-layouts  5.13 us

profile of v2, /device:TPU:1, one launch (start us, length us, event | category | flops | bytes accessed | tf_op | source)
XLA Modules:
  0.0 129.3 jit_solution(1695810199503580441)
XLA Ops:
  0.0 0.0 copy-start.3
  0.0 0.7 copy-done.3
  0.7 0.0 copy-start
  0.7 1.2 copy-done
  1.9 0.0 copy-start.1
  1.9 1.0 copy-done.1
  3.0 0.0 copy-start.2
  3.0 0.7 copy-done.2
  3.7 0.0 copy-start.4
  3.7 0.7 copy-done.4
  4.3 124.2 %shard_map.55 = bf16[2,64,16,128]{3,2,1,0:T(8,128)(2,1)S(1)} custom-call(s32[1,1024]{1,0:T(1,128)S(1)} %bitcast.6, s32[1,1024]{1,0:T(1,128)S(1)} %bitcast.7, s32[16,16]{1,0:T(8,128)S(1)} %bitcast.5, bf16[2,1024,128]{2,1,0:T(8,128)(2,1)S(1)} %copy-done.1, bf16[256,2048]{1,0:T(8,128)(2,1)S(1)} %bitcast.4), custom_call_target="tpu_custom_call" | custom-call | tf_op jit(solution)/shard_map/pallas_call | solution.py:385
  128.5 0.8 copy.7
Async XLA Ops:
  0.0 0.7 copy-start.3
  0.7 1.2 copy-start
  1.9 1.0 copy-start.1
  3.0 0.7 copy-start.2
  3.7 0.7 copy-start.4

commit v3 on v2

v3 whole, which is shorter than its diff:
```python
import functools

import jax
import jax.numpy as jnp
from jax import lax
from jax.experimental import pallas as pl
from jax.experimental.pallas import tpu as pltpu
from jax.sharding import PartitionSpec as P

MESH = pl.DeviceIdType.MESH
CORES = 2
RING = 4
ROW = CORES * RING
RELAY = 128
HALVES = 2
LAG = 7


def one_hot_bf16(cond):
    return jnp.where(cond, 1.0, 0.0).astype(jnp.bfloat16)


def kernel(
    n_pair,
    n_slab,
    owner_hbm,
    sym_hbm,
    screen_hbm,
    amps_hbm,
    b_hbm,
    out_ref,
    owner_ref,
    sym_ref,
    screen_ref,
    amps_ref,
    send_a,
    recv_a,
    a_mat,
    f32_a,
    f32_c,
    acc,
    spread_b,
    gathered,
    coupling,
    mask_ref,
    send_c,
    load_sem,
    x_send,
    x_recv,
    y_send,
    y_recv,
    side_send,
    side_recv,
    relay_send,
    relay_recv,
    twin_send,
    twin_recv,
    screen_send,
    screen_recv,
    a_send,
    a_recv,
    c_send,
    c_recv,
):
    pair = lax.axis_index("pair")
    slab = lax.axis_index("slab")
    rows, tiles, width = amps_hbm.shape
    per = tiles // n_pair
    depth, cols = b_hbm.shape
    half = cols // HALVES
    block = half // RING
    layer = pair // ROW
    ring = lax.rem(pair // CORES, RING)
    core = lax.rem(pair, CORES)
    row_base = layer * ROW

    home = ring + RING * core
    at_home = home == slab
    served = row_base + lax.rem(slab, RING) * CORES + slab // RING
    spot = layer * n_slab + slab

    loads = [
        pltpu.make_async_copy(src, dst, load_sem.at[i])
        for i, (src, dst) in enumerate(
            ((owner_hbm, owner_ref), (sym_hbm, sym_ref), (screen_hbm, screen_ref), (amps_hbm, amps_ref))
        )
    ]
    for load in loads:
        load.start()

    def device_at(x, c):
        return row_base + x * CORES + c

    def in_row(i):
        return row_base + lax.rem(pair - row_base + i, ROW)

    def spread_over(i):
        other = lax.rem(spot + i, n_pair)
        there = other // n_slab
        return there * ROW + pair - row_base, lax.rem(other, n_slab)

    twin = device_at(ring, 1 - core)
    right = device_at(lax.rem(ring + 1, RING), core)
    left = device_at(lax.rem(ring + RING - 1, RING), core)

    barrier = pltpu.get_barrier_semaphore()

    def greet(device):
        pl.semaphore_signal(barrier, inc=1, device_id=device, device_id_type=MESH)

    for i in range(1, ROW):
        greet((in_row(i), slab))
    for i in range(1, n_slab):
        greet((twin, lax.rem(slab + i, n_slab)))

    @pl.loop(1, n_pair)
    def _(i):
        greet(spread_over(i))

    pl.semaphore_wait(barrier, n_pair - 1 + ROW - 1 + n_slab - 1)

    def x_source(u, to):
        return b_hbm.at[:, pl.ds(pl.multiple_of(u * half + to * block, block), block)]

    def x_copy(u, i):
        to = lax.rem(ring + i, RING)
        return pltpu.make_async_remote_copy(
            src_ref=x_source(u, to),
            dst_ref=spread_b.at[u, ring],
            send_sem=x_send.at[u],
            recv_sem=x_recv.at[u, ring],
            device_id=(device_at(to, core), slab),
            device_id_type=MESH,
        )

    for u in range(HALVES):
        for i in (1, 3, 2):
            x_copy(u, i).start()
        pltpu.make_async_copy(x_source(u, ring), spread_b.at[u, ring], x_recv.at[u, ring]).start()

    def y_step(u):
        for i in range(RING):
            x0 = lax.rem(ring + i, RING)
            pltpu.make_async_copy(spread_b.at[u, x0], spread_b.at[u, x0], x_recv.at[u, x0]).wait()
            there = x0 + RING * core
            for swap in range(CORES):
                h = lax.rem(core + swap, CORES)
                src = spread_b.at[u, x0, :, pl.ds(pl.multiple_of(h * width, width), width)]
                dst = gathered.at[u, h, slab, ring]
                far = pltpu.make_async_remote_copy(
                    src_ref=src,
                    dst_ref=dst,
                    send_sem=y_send.at[u],
                    recv_sem=y_recv.at[u, slab],
                    device_id=(device_at(ring, h), there),
                    device_id_type=MESH,
                )
                if swap:
                    far.start()
                else:
                    near = pltpu.make_async_copy(src, dst, y_recv.at[u, slab])

                    @pl.when(there == slab)
                    def _():
                        near.start()

                    @pl.when(there != slab)
                    def _():
                        far.start()

    order = [0]
    for k in range(1, n_slab // 2):
        order += [k, n_slab - k]
    order += [n_slab // 2]

    def at(t):
        return t // n_slab, lax.rem(slab + order[t % n_slab], n_slab)

    def remote(ref, send, recv, to):
        return pltpu.make_async_remote_copy(
            src_ref=ref, dst_ref=ref, send_sem=send, recv_sem=recv, device_id=(to, slab), device_id_type=MESH
        )

    def side(t, way):
        u, y = at(t)
        ref = gathered.at[u, core, y, ring]
        return remote(ref, side_send.at[way, t], side_recv.at[way, t], (right, left)[way])

    def relay(t, way):
        u, y = at(t)
        x0 = lax.rem(ring + (RING - 1 if way == 0 else 1), RING)
        part = pl.ds(0, RELAY) if way == 0 else pl.ds(RELAY, depth - RELAY)
        ref = gathered.at[u, core, y, x0, part]
        return remote(ref, relay_send.at[way, t], relay_recv.at[way, t], (right, left)[way])

    def arrived_side(t, way):
        u, y = at(t)
        x0 = lax.rem(ring + (RING - 1 if way == 0 else 1), RING)
        ref = gathered.at[u, core, y, x0]
        return pltpu.make_async_copy(ref, ref, side_recv.at[way, t])

    def across(t):
        u, y = at(t)
        return remote(gathered.at[u, core, y], twin_send.at[t], twin_recv.at[t], twin)

    def stage0(t):
        u, y = at(t)
        ref = gathered.at[u, core, y, ring]
        pltpu.make_async_copy(ref, ref, y_recv.at[u, y]).wait()
        side(t, 0).start()
        side(t, 1).start()

    def stage1(t):
        arrived_side(t, 0).wait()
        relay(t, 0).start()
        arrived_side(t, 1).wait()
        relay(t, 1).start()

    def stage2(t):
        relay(t, 0).wait_recv()
        relay(t, 1).wait_recv()
        across(t).start()

    for load in loads:
        load.wait()
    owned = owner_ref[...]
    sel = lax.broadcasted_iota(jnp.int32, (n_pair, tiles), 0) == owned
    sel_bf = one_hot_bf16(sel)
    count = jnp.zeros((n_pair, tiles), jnp.float32)
    span = 256
    for part in range(tiles // span):
        before = lax.broadcasted_iota(jnp.int32, (span, tiles), 0) + part * span < lax.broadcasted_iota(
            jnp.int32, (span, tiles), 1
        )
        count += jnp.dot(
            sel_bf[:, part * span : (part + 1) * span], one_hot_bf16(before), preferred_element_type=jnp.float32
        )
    base = (lax.broadcasted_iota(jnp.int32, (n_pair, tiles), 0) * per).astype(jnp.float32)
    rank = jnp.sum(jnp.where(sel, count + base, 0.0), axis=0, keepdims=True).astype(jnp.int32)

    flat = jnp.concatenate([amps_ref[o] for o in range(rows)], axis=1)
    for part in range(tiles // span):
        pick = one_hot_bf16(lax.broadcasted_iota(jnp.int32, (span, tiles), 0) + part * span == rank)
        got = jnp.dot(pick, flat, preferred_element_type=jnp.float32).astype(jnp.bfloat16)
        first = part * span // per
        for o in range(rows):
            send_a[first : first + span // per, o] = got[:, o * width : (o + 1) * width].reshape(
                span // per, per, width
            )

    def a_copy(i):
        to, there = spread_over(i)
        wanted = to - (pair - row_base) + lax.rem(there, RING) * CORES + there // RING
        return pltpu.make_async_remote_copy(
            src_ref=send_a.at[wanted],
            dst_ref=recv_a.at[spot],
            send_sem=a_send,
            recv_sem=a_recv,
            device_id=(to, there),
            device_id_type=MESH,
        )

    y_step(0)

    @pl.loop(1, n_pair)
    def _(i):
        a_copy(i).start()

    y_step(1)
    recv_a[spot] = send_a[served]

    def screen_copy(i):
        return pltpu.make_async_remote_copy(
            src_ref=coupling,
            dst_ref=coupling,
            send_sem=screen_send,
            recv_sem=screen_recv,
            device_id=(in_row(i), slab),
            device_id_type=MESH,
        )

    @pl.when(at_home)
    def _():
        coupling[...] = jnp.zeros_like(coupling)
        coupling[:, :per] = jnp.where(screen_ref[...] == 1, 1.0, 0.0)

        @pl.loop(1, ROW)
        def _(i):
            screen_copy(i).start()

    @pl.when(jnp.logical_not(at_home))
    def _():
        screen_copy(0).wait_recv()

    mine = one_hot_bf16(lax.broadcasted_iota(jnp.int32, (per, tiles), 0) + served * per == rank)
    classes = lax.broadcasted_iota(jnp.int32, (128, tiles), 0) == sym_ref[...]
    labels = lax.dot_general(
        mine, one_hot_bf16(classes), (((1,), (1,)), ((), ())), preferred_element_type=jnp.float32
    ).astype(jnp.bfloat16)
    same = lax.dot_general(labels, labels, (((1,), (1,)), ((), ())), preferred_element_type=jnp.float32)
    allowed = (coupling[:, :per] * same).astype(jnp.bfloat16)
    spread = one_hot_bf16(
        lax.broadcasted_iota(jnp.int32, (per, cols), 0) == lax.broadcasted_iota(jnp.int32, (per, cols), 1) // width
    )
    mask_ref[...] = jnp.dot(allowed, spread, preferred_element_type=jnp.float32)

    held = n_pair * rows

    def all_of(ref, sem):
        part = ref.at[pl.ds(0, n_pair - 1)]
        return pltpu.make_async_copy(part, part, sem)

    def arrange():
        all_of(recv_a, a_recv).wait()
        f32_a[...] = recv_a[...].reshape(held * per, width).astype(jnp.float32)
        for k in range(per):
            a_mat[k // 2, :, (k % 2) * width : (k % 2 + 1) * width] = f32_a[
                pl.ds(k, held, stride=per), :
            ].astype(jnp.bfloat16)

    deep = depth // width
    part_l = per // HALVES

    def multiply(t):
        u, y = at(t)
        across(t).wait_recv()
        lhs = a_mat[y]
        for q in range(RING):
            start = u * half + q * block
            term = []
            for part in range(deep):
                row = mask_ref[pl.ds(y * deep + part, 1), start : start + block]
                span_k = slice(part * width, (part + 1) * width)
                both = jnp.concatenate([gathered[u, h, y, q, span_k, :] for h in range(CORES)], axis=1)
                term.append(both * row.astype(jnp.bfloat16))
            prod = jnp.dot(lhs, jnp.concatenate(term, axis=0), preferred_element_type=jnp.float32)
            where = slice(q * block, (q + 1) * block)
            k = t % n_slab
            if k:
                prod = acc[:, where] + prod
            if k < n_slab - 1:
                acc[:, where] = prod
            else:
                for h in range(CORES):
                    f32_c[pl.ds(q * CORES + h, held, stride=part_l), :] = prod[:, h * width : (h + 1) * width]

    def c_copy(u, i):
        return pltpu.make_async_remote_copy(
            src_ref=send_c.at[u, lax.rem(spot + i, n_pair)],
            dst_ref=out_ref.at[:, served, u],
            send_sem=c_send.at[u],
            recv_sem=c_recv.at[u],
            device_id=spread_over(i),
            device_id_type=MESH,
        )

    def give_back(u):
        send_c[u] = f32_c[...].astype(jnp.bfloat16).reshape(n_pair, rows, part_l, width)

        @pl.loop(1, n_pair)
        def _(i):
            c_copy(u, i).start()

        out_ref[:, served, u] = send_c[u, spot]

    steps = HALVES * n_slab
    done = 0
    for t in range(steps + 2):
        if t < steps:
            stage0(t)
        if 0 <= t - 1 < steps:
            stage1(t - 1)
        if 0 <= t - 2:
            stage2(t - 2)
        if t == LAG:
            arrange()
        if t >= LAG:
            for _ in range(2):
                if done <= t - 3:
                    multiply(done)
                    done += 1
                    if done % n_slab == 0:
                        give_back(done // n_slab - 1)
    while done < steps:
        multiply(done)
        done += 1
        if done % n_slab == 0:
            give_back(done // n_slab - 1)

    for u in range(HALVES):
        sent = spread_b.at[u, pl.ds(0, RING - 1)]
        pltpu.make_async_copy(sent, sent, x_send.at[u]).wait()
        some = gathered.at[u, 0, pl.ds(0, 1)]
        pltpu.make_async_copy(some, some, y_send.at[u]).wait()
        rest = gathered.at[u, 0, 0, pl.ds(0, RING - 1)]
        pltpu.make_async_copy(rest, rest, y_send.at[u]).wait()

    @pl.when(slab // RING != core)
    def _():
        for u in range(HALVES):
            one = gathered.at[u, 0, 0, 0]
            pltpu.make_async_copy(one, one, y_send.at[u]).wait()

    @pl.when(at_home)
    def _():
        @pl.loop(1, ROW)
        def _(i):
            screen_copy(i).wait_send()

    for t in range(steps):
        for way in range(2):
            side(t, way).wait_send()
            relay(t, way).wait_send()
        across(t).wait_send()
    all_of(send_a, a_send).wait()

    def result_bytes(u, sem):
        part = send_c.at[u, pl.ds(0, n_pair - 1)]
        return pltpu.make_async_copy(part, part, sem)

    for u in range(HALVES):
        result_bytes(u, c_send.at[u]).wait()
        result_bytes(u, c_recv.at[u]).wait()


def on_device(amps, symmetry, screen, owner, integrals):
    n_pair, n_slab = lax.axis_size("pair"), lax.axis_size("slab")
    rows, tiles, width = amps.shape
    per = tiles // n_pair
    depth, cols = integrals.shape[1:]
    block = cols // HALVES // RING
    held = n_pair * rows
    steps = HALVES * n_slab
    bf16, f32 = jnp.bfloat16, jnp.float32
    dma = pltpu.SemaphoreType.DMA
    result = pl.pallas_call(
        functools.partial(kernel, n_pair, n_slab),
        out_shape=jax.ShapeDtypeStruct((rows, n_pair, HALVES, per // HALVES, width), bf16),
        in_specs=[pl.BlockSpec(memory_space=pltpu.HBM)] * 5,
        out_specs=pl.BlockSpec(memory_space=pltpu.VMEM),
        scratch_shapes=[
            pltpu.VMEM((1, tiles), jnp.int32),
            pltpu.VMEM((1, tiles), jnp.int32),
            pltpu.VMEM((per, per), jnp.int32),
            pltpu.VMEM((rows, tiles, width), bf16),
            pltpu.VMEM((n_pair, rows, per, width), bf16),
            pltpu.VMEM((n_pair, rows, per, width), bf16),
            pltpu.VMEM((n_slab, held, depth), bf16),
            pltpu.VMEM((held * per, width), f32),
            pltpu.VMEM((held * per // HALVES, width), f32),
            pltpu.VMEM((held, cols // HALVES), f32),
            pltpu.VMEM((HALVES, RING, depth, block), bf16),
            pltpu.VMEM((HALVES, CORES, n_slab, RING, depth, block // CORES), bf16),
            pltpu.VMEM((per, 128), f32),
            pltpu.VMEM((per, cols), f32),
            pltpu.VMEM((HALVES, n_pair, rows, per // HALVES, width), bf16),
            dma((4,)),
            dma((HALVES,)),
            dma((HALVES, RING)),
            dma((HALVES,)),
            dma((HALVES, n_slab)),
            dma((2, steps)),
            dma((2, steps)),
            dma((2, steps)),
            dma((2, steps)),
            dma((steps,)),
            dma((steps,)),
            dma,
            dma,
            dma,
            dma,
            dma((HALVES,)),
            dma((HALVES,)),
        ],
        compiler_params=pltpu.CompilerParams(
            collective_id=0, has_side_effects=True, vmem_limit_bytes=63 << 20
        ),
    )(owner[None, :], symmetry[None, :], screen[0], amps, integrals[0])
    return result.reshape(rows, n_pair, per, width)


def solution(mesh):
    in_specs = (
        P(("pair", "slab"), None, None),
        P(),
        P("pair", None, None),
        P(),
        P("pair", "slab", None),
    )
    out_specs = P(("pair", "slab"), None, None, None)
    return jax.shard_map(
        on_device, mesh=mesh, in_specs=in_specs, out_specs=out_specs, check_vma=False
    )
```

time: 130 us -> 101 us (0.78)
  Pallas kernels: 124 us -> 99.2 us
  local copies, waits for them, and re-layouts: 5.13 us -> 1.87 us
    pallas_call x1, Pallas kernels: 124 us -> 99.2 us  [on_device(): pl.pallas_call(functools.partial(kernel, n_pair, n_slab), out_shape=jax.S...]
    unnamed x11 -> x1, local copies, waits for them, and re-layouts: 5.13 us -> 1.87 us
where the time goes in v3:
time: 101 us
  Pallas kernels  99.2 us (98%)
  local copies, waits for them, and re-layouts  1.87 us (2%)
    pallas_call x1, Pallas kernels, on_device(): pl.pallas_call(functools.partial(kernel, n_pair, n_slab), out_shape=jax.S...  99.2 us

profile of v3, /device:TPU:1, one launch (start us, length us, event | category | flops | bytes accessed | tf_op | source)
XLA Modules:
  0.0 101.1 jit_solution(7894703976022218154)
XLA Ops:
  0.0 99.2 %shard_map.55 = bf16[2,64,2,8,128]{4,3,2,1,0:T(8,128)(2,1)} custom-call(s32[1,1024]{1,0:T(1,128)} %bitcast.8, s32[1,1024]{1,0:T(1,128)} %bitcast.9, s32[16,16]{1,0:T(8,128)} %bitcast.7, bf16[2,1024,128]{2,1,0:T(8,128)(2,1)} %amps_hbm.1, bf16[256,2048]{1,0:T(8,128)(2,1)} %bitcast.6), custom_call_target="tpu_custom_call" | custom-call | tf_op jit(solution)/shard_map/pallas_call | solution.py:436
  99.2 1.9 %copy.7 = bf16[2,64,16,128]{3,2,1,0:T(8,128)(2,1)} copy(bf16[2,64,16,128]{3,2,1,0:T(8,128)(2,1)} %bitcast.5) | data formatting | bytes 1048576

commit v4 on v3

--- a/solution.py
+++ b/solution.py
@@ -13,7 +13,10 @@
 ROW = CORES * RING
 RELAY = 128
 HALVES = 2
-LAG = 7
+LAG = 11
+AHEAD = 8
+SIDE_LAG = 3
+FAR_LAG = 6
 
 
 def one_hot_bf16(cond):
@@ -133,40 +136,12 @@
             device_id_type=MESH,
         )
 
-    for u in range(HALVES):
+    def x_step(u):
         for i in (1, 3, 2):
             x_copy(u, i).start()
         pltpu.make_async_copy(x_source(u, ring), spread_b.at[u, ring], x_recv.at[u, ring]).start()
 
-    def y_step(u):
-        for i in range(RING):
-            x0 = lax.rem(ring + i, RING)
-            pltpu.make_async_copy(spread_b.at[u, x0], spread_b.at[u, x0], x_recv.at[u, x0]).wait()
-            there = x0 + RING * core
-            for swap in range(CORES):
-                h = lax.rem(core + swap, CORES)
-                src = spread_b.at[u, x0, :, pl.ds(pl.multiple_of(h * width, width), width)]
-                dst = gathered.at[u, h, slab, ring]
-                far = pltpu.make_async_remote_copy(
-                    src_ref=src,
-                    dst_ref=dst,
-                    send_sem=y_send.at[u],
-                    recv_sem=y_recv.at[u, slab],
-                    device_id=(device_at(ring, h), there),
-                    device_id_type=MESH,
-                )
-                if swap:
-                    far.start()
-                else:
-                    near = pltpu.make_async_copy(src, dst, y_recv.at[u, slab])
-
-                    @pl.when(there == slab)
-                    def _():
-                        near.start()
-
-                    @pl.when(there != slab)
-                    def _():
-                        far.start()
+    x_step(0)
 
     order = [0]
     for k in range(1, n_slab // 2):
@@ -175,6 +150,32 @@
 
     def at(t):
         return t // n_slab, lax.rem(slab + order[t % n_slab], n_slab)
+
+    def x_arrived(u):
+        for x0 in range(RING):
+            pltpu.make_async_copy(spread_b.at[u, x0], spread_b.at[u, x0], x_recv.at[u, x0]).wait()
+
+    def y_step(t):
+        u, k = t // n_slab, t % n_slab
+        there = lax.rem(slab + n_slab - order[k], n_slab)
+
+        @pl.when(there // RING == core)
+        def _():
+            for swap in range(CORES):
+                h = lax.rem(core + swap, CORES)
+                src = spread_b.at[u, lax.rem(there, RING), :, pl.ds(pl.multiple_of(h * width, width), width)]
+                dst = gathered.at[u, h, slab, ring]
+                if k == 0 and swap == 0:
+                    pltpu.make_async_copy(src, dst, y_recv.at[u, slab]).start()
+                else:
+                    pltpu.make_async_remote_copy(
+                        src_ref=src,
+                        dst_ref=dst,
+                        send_sem=y_send.at[u],
+                        recv_sem=y_recv.at[u, slab],
+                        device_id=(device_at(ring, h), there),
+                        device_id_type=MESH,
+                    ).start()
 
     def remote(ref, send, recv, to):
         return pltpu.make_async_remote_copy(
@@ -260,13 +261,14 @@
             device_id_type=MESH,
         )
 
-    y_step(0)
-
     @pl.loop(1, n_pair)
     def _(i):
         a_copy(i).start()
 
-    y_step(1)
+    x_arrived(0)
+    for t in range(AHEAD):
+        y_step(t)
+    x_step(1)
     recv_a[spot] = send_a[served]
 
     def screen_copy(i):
@@ -365,18 +367,22 @@
 
     steps = HALVES * n_slab
     done = 0
-    for t in range(steps + 2):
+    for t in range(steps + FAR_LAG):
         if t < steps:
             stage0(t)
-        if 0 <= t - 1 < steps:
-            stage1(t - 1)
-        if 0 <= t - 2:
-            stage2(t - 2)
+        if t + AHEAD < steps:
+            if t + AHEAD == n_slab:
+                x_arrived(1)
+            y_step(t + AHEAD)
+        if 0 <= t - SIDE_LAG < steps:
+            stage1(t - SIDE_LAG)
+        if 0 <= t - FAR_LAG < steps:
+            stage2(t - FAR_LAG)
         if t == LAG:
             arrange()
         if t >= LAG:
             for _ in range(2):
-                if done <= t - 3:
+                if done < t - FAR_LAG:
                     multiply(done)
                     done += 1
                     if done % n_slab == 0:

time: 101 us -> 87.7 us (0.87)
  Pallas kernels: 99.2 us -> 85.6 us
    pallas_call x1, Pallas kernels: 99.2 us -> 85.6 us  [on_device(): pl.pallas_call(functools.partial(kernel, n_pair, n_slab), out_shape=jax.S...]
where the time goes in v4:
time: 87.7 us; the launch traced here: 87.5 us
  Pallas kernels  85.6 us (98%)
  local copies, waits for them, and re-layouts  1.87 us (2%)
    pallas_call x1, Pallas kernels, on_device(): pl.pallas_call(functools.partial(kernel, n_pair, n_slab), out_shape=jax.S...  85.6 us
    unnamed x1, local copies, waits for them, and re-layouts  1.87 us

profile of v4, /device:TPU:1, one launch (start us, length us, event | category | flops | bytes accessed | tf_op | source)
XLA Modules:
  0.0 87.5 jit_solution(7196278492570182887)
XLA Ops:
  0.0 85.6 %shard_map.55 = bf16[2,64,2,8,128]{4,3,2,1,0:T(8,128)(2,1)} custom-call(s32[1,1024]{1,0:T(1,128)} %bitcast.8, s32[1,1024]{1,0:T(1,128)} %bitcast.9, s32[16,16]{1,0:T(8,128)} %bitcast.7, bf16[2,1024,128]{2,1,0:T(8,128)(2,1)} %amps_hbm.1, bf16[256,2048]{1,0:T(8,128)(2,1)} %bitcast.6), custom_call_target="tpu_custom_call" | custom-call | tf_op jit(solution)/shard_map/pallas_call | solution.py:442
  85.6 1.9 %copy.7 = bf16[2,64,16,128]{3,2,1,0:T(8,128)(2,1)} copy(bf16[2,64,16,128]{3,2,1,0:T(8,128)(2,1)} %bitcast.5) | data formatting | bytes 1048576

commit v5 on v4

--- a/solution.py
+++ b/solution.py
@@ -14,7 +14,8 @@
 RELAY = 128
 HALVES = 2
 LAG = 11
-AHEAD = 8
+FIRST = 8
+ISSUE = {2: (8, 12), 5: (12, 16)}
 SIDE_LAG = 3
 FAR_LAG = 6
 
@@ -266,7 +267,7 @@
         a_copy(i).start()
 
     x_arrived(0)
-    for t in range(AHEAD):
+    for t in range(FIRST):
         y_step(t)
     x_step(1)
     recv_a[spot] = send_a[served]
@@ -370,10 +371,10 @@
     for t in range(steps + FAR_LAG):
         if t < steps:
             stage0(t)
-        if t + AHEAD < steps:
-            if t + AHEAD == n_slab:
+        for r in range(*ISSUE.get(t, (0, 0))):
+            if r == n_slab:
                 x_arrived(1)
-            y_step(t + AHEAD)
+            y_step(r)
         if 0 <= t - SIDE_LAG < steps:
             stage1(t - SIDE_LAG)
         if 0 <= t - FAR_LAG < steps:

time: 87.7 us -> 87.6 us (level)
  no operation moved by 1% of the time
where the time goes in v5:
time: 87.6 us; the launch traced here: 87.5 us
  Pallas kernels  85.6 us (98%)
  local copies, waits for them, and re-layouts  1.87 us (2%)
    pallas_call x1, Pallas kernels, on_device(): pl.pallas_call(functools.partial(kernel, n_pair, n_slab), out_shape=jax.S...  85.6 us
    unnamed x1, local copies, waits for them, and re-layouts  1.87 us

profile of v5, /device:TPU:1, one launch (start us, length us, event | category | flops | bytes accessed | tf_op | source)
XLA Modules:
  0.0 87.5 jit_solution(2506851771035112077)
XLA Ops:
  0.0 85.6 %shard_map.55 = bf16[2,64,2,8,128]{4,3,2,1,0:T(8,128)(2,1)} custom-call(s32[1,1024]{1,0:T(1,128)} %bitcast.8, s32[1,1024]{1,0:T(1,128)} %bitcast.9, s32[16,16]{1,0:T(8,128)} %bitcast.7, bf16[2,1024,128]{2,1,0:T(8,128)(2,1)} %amps_hbm.1, bf16[256,2048]{1,0:T(8,128)(2,1)} %bitcast.6), custom_call_target="tpu_custom_call" | custom-call | tf_op jit(solution)/shard_map/pallas_call | solution.py:443
  85.6 1.9 %copy.7 = bf16[2,64,16,128]{3,2,1,0:T(8,128)(2,1)} copy(bf16[2,64,16,128]{3,2,1,0:T(8,128)(2,1)} %bitcast.5) | data formatting | bytes 1048576
